TPU v7x, 768 devices: a whole 4x8x12 slice. The times are simulated.
768 devices in a mesh: block: 48 (over y, z_lo), chan: 16 (over x, z_hi, core).
Axes of the slice: x: 4, y: 8, z: 12 (z_hi: 2, z_lo: 6; z = z_hi * 6 + z_lo), core: 2. Of those that a mesh axis runs over, the one named last changes fastest.
Arguments:
- volume: bfloat16 [16, 192, 64, 128], P(None, 'block', 'chan'), may hold values from -6 to 6
- kernel: bfloat16 [32, 27, 16], replicated, may hold values from -0.3125 to 0.3125
- conv_bias: float32 [32], replicated, may hold values from -0.5 to 0.5
- pooled_grad: bfloat16 [32, 96, 32, 64], P(None, 'block', 'chan'), may hold values from -40 to 40
Outputs:
- pooled: bfloat16 [32, 96, 32, 64], P(None, 'block', 'chan')
- volume_grad: bfloat16 [16, 192, 64, 128], P(None, 'block', 'chan')
- kernel_grad: float32 [32, 27, 16], replicated
- bias_grad: float32 [32], replicated
All inputs are finite; a program needn't handle non-finite values.
Results may differ from a plain program's by a relative error of at most 0.005.
Values may be sent and summed in bfloat16 or wider, within the bound.
A program may use at most 32 MiB of HBM per device.

v0:
```python
import jax
import jax.numpy as jnp
from jax import lax
from jax.sharding import PartitionSpec as P


def extended(shard, sides, width):
    for axis, dim in sides:
        count, length = (lax.axis_size(axis), shard.shape[dim])
        up = [(i, (i + 1) % count) for i in range(count - 1)]
        down = [(j, i) for i, j in up]
        last = lax.slice_in_dim(shard, length - width, length, axis=dim)
        initial = lax.slice_in_dim(shard, 0, width, axis=dim)
        before = lax.ppermute(last, axis, up)
        after = lax.ppermute(initial, axis, down)
        shard = jnp.concatenate([before, shard, after], axis=dim)
    return shard


def conv_valid(inputs, filters):
    return lax.conv_general_dilated(
        inputs[None],
        filters,
        (1, 1, 1),
        ((0, 0), (0, 0), (1, 1)),
        dimension_numbers=("NCDHW", "OIDHW", "NCDHW"),
        preferred_element_type=jnp.float32,
    )[0]


def upsample(coarse):
    return jnp.repeat(jnp.repeat(jnp.repeat(coarse, 2, 1), 2, 2), 2, 3)


def forward_local(widened, fwd_filters, conv_bias, pooled_grad):
    preact = conv_valid(widened, fwd_filters) + conv_bias[:, None, None, None]
    slope = 0.2 + 0.8 * jax.nn.sigmoid(preact)
    pre_grad = (upsample(pooled_grad).astype(jnp.float32) * 0.125 * slope).astype(jnp.bfloat16)
    return (preact, pre_grad)


def local(volume, kernel, conv_bias, pooled_grad):
    in_chan, row_count, col_count, deep_count = volume.shape
    out_chan = kernel.shape[0]
    weights = kernel.reshape(out_chan, 3, 3, 3, in_chan)
    fwd_filters = weights.transpose(0, 4, 1, 2, 3)
    back_filters = weights[:, ::-1, ::-1, ::-1, :].transpose(4, 0, 1, 2, 3)
    widened = extended(volume, (("block", 1), ("chan", 2)), 1)
    preact, pre_grad = forward_local(widened, fwd_filters, conv_bias, pooled_grad)
    grad_wide = extended(pre_grad, (("block", 1), ("chan", 2)), 1)
    smooth = 0.2 * preact + 0.8 * jax.nn.softplus(preact)
    pooled = (
        smooth.reshape(out_chan, row_count // 2, 2, col_count // 2, 2, deep_count // 2, 2)
        .mean(axis=(2, 4, 6))
        .astype(jnp.bfloat16)
    )
    volume_grad = conv_valid(grad_wide, back_filters).astype(jnp.bfloat16)
    deep_padded = jnp.pad(widened, ((0, 0), (0, 0), (0, 0), (1, 1)))
    local_kernel = lax.conv_general_dilated(
        deep_padded[:, None],
        pre_grad[:, None],
        (1, 1, 1),
        ((0, 0), (0, 0), (0, 0)),
        dimension_numbers=("NCDHW", "OIDHW", "NCDHW"),
        preferred_element_type=jnp.float32,
    )
    local_kernel = local_kernel.transpose(1, 2, 3, 4, 0).reshape(out_chan, 27, in_chan)
    local_bias = jnp.sum(pre_grad.astype(jnp.float32), axis=(1, 2, 3))
    kernel_grad, bias_grad = lax.psum((local_kernel, local_bias), ("block", "chan"))
    return (pooled, volume_grad, kernel_grad, bias_grad)


def solution(mesh):
    placed = (P(None, "block", "chan", None), P(), P(), P(None, "block", "chan", None))
    return jax.shard_map(
        local,
        mesh=mesh,
        in_specs=placed,
        out_specs=(P(None, "block", "chan", None), P(None, "block", "chan", None), P(), P()),
        check_vma=False,
    )
```

profile of v0, /device:TPU:1, one launch (start us, length us, event | category | flops | bytes accessed | tf_op | source)
XLA Modules:
  0.0 216.8 jit_solution(8771547578564711794)
XLA Ops:
  0.6 0.8 fusion.51
  1.4 4.8 %collective-permute-start = (bf16[16,1,4,128]{3,0,2,1:T(8,128)(2,1)S(1)}, bf16[16,1,4,128]{3,0,2,1:T(8,128)(2,1)S(1)}, u32[]{:S(2)}, u32[]{:S(2)}) collective-permute-start(bf16[16,1,4,128]{3,0,2,1:T(8,128)(2,1)S(1)} %copy.97), channel_id=1, source_target_pairs={{0,16},{16,32},{32,48},{48,64},{64,80},{80,96},{96,112},{112,128},... | collective-permute-start | bytes 49160 | tf_op jit(solution)/shard_map/ppermute | solution.py:14
  6.3 1.3 collective-permute-start.1
  7.6 0.9 copy.76
  8.5 0.9 constant_dynamic-update-slice_fusion.1
  9.4 2.1 collective-permute-done.1
  11.4 15.9 %collective-permute-start.2 = (bf16[16,6,1,128]{3,0,2,1:T(8,128)(2,1)S(1)}, bf16[16,6,1,128]{3,0,2,1:T(8,128)(2,1)S(1)}, u32[]{:S(2)}, u32[]{:S(2)}) collective-permute-start(bf16[16,6,1,128]{3,0,2,1:T(8,128)(2,1)S(1)} %get-tuple-element.28), channel_id=1, source_target_pairs={{0,1},{1,2},{2,3},{3,4},{4,5},{5,6},{6,7},{7,8},{8,9},{9,10},{10,1... | collective-permute-start | bytes 73736 | tf_op jit(solution)/shard_map/ppermute | solution.py:14
  27.4 1.9 collective-permute-start.3
  30.2 1.0 copy.78
  31.2 1.0 copy.83
  32.2 6.6 %collective-permute-done.3 = bf16[16,6,1,128]{3,0,2,1:T(8,128)(2,1)S(1)} collective-permute-done((bf16[16,6,1,128]{3,0,2,1:T(8,128)(2,1)S(1)}, bf16[16,6,1,128]{3,0,2,1:T(8,128)(2,1)S(1)}, u32[]{:S(2)}, u32[]{:S(2)}) %collective-permute-start.3) | collective-permute-done | bytes 24608 | tf_op jit(solution)/shard_map/ppermute | solution.py:15
  39.0 0.8 reshape.100
  39.9 2.0 copy.71
  42.0 3.0 %multiply_add_fusion = (f32[4,4,8,17,32]{4,2,3,1,0:T(8,128)}, f32[4,4,8,17,32]{4,2,3,1,0:T(8,128)S(1)}) fusion(f32[32]{0:T(128)S(1)} %copy-done.6, bf16[32,3,3,3,16]{0,4,3,2,1:T(8,128)(2,1)S(1)} %bitcast.96, bf16[16,6,6,1,7,2]{0,4,5,2,1,3:T(8,128)(2,1)S(1)} %slice.41, bf16[16,6,6,1,8,17]{0,4,5,2,1,3:T(8,128)(2,1)S(1)} %copy.71, pred[8,17]{0,1:T(8,128)(4,1)S(1)} %copy-done.8), kind=kOutput, calls=%fused_computation.18 | convolution fusion | flops 61174784 | bytes 757768 | tf_op jit(solution)/shard_map/conv_general_dilated | solution.py:21
  46.0 0.7 copy-done.3
  47.0 4.0 %fusion.23 = f32[32,2,2,64]{0,3,2,1:T(8,128)} fusion(f32[32,2,2,2,2,64,2]{0,6,5,4,3,2,1:T(2,128)S(1)} %bitcast.104, f32[32]{0:T(128)S(1)} %copy-done.6), kind=kLoop, calls=%fused_computation.26 | loop fusion | flops 712704 | bytes 295040 | tf_op jit(solution)/shard_map/reduce_sum | solution.py:54
  50.9 0.6 fusion.49
  51.6 3.7 %collective-permute-start.4 = (bf16[32,1,4,128]{3,0,2,1:T(8,128)(2,1)}, bf16[32,1,4,128]{3,0,2,1:T(8,128)(2,1)S(1)}, u32[]{:S(2)}, u32[]{:S(2)}) collective-permute-start(bf16[32,1,4,128]{3,0,2,1:T(8,128)(2,1)} %get-tuple-element.26), channel_id=1, source_target_pairs={{0,16},{16,32},{32,48},{48,64},{64,80},{80,96},{96,112},{112,128},... | collective-permute-start | bytes 98312 | tf_op jit(solution)/shard_map/ppermute | solution.py:14
  55.3 1.3 collective-permute-start.5
  56.6 2.0 copy.85
  58.6 2.7 %copy.84 = bf16[16,1,6,6,130]{0,1,4,3,2:T(2,128)(2,1)S(1)} copy(bf16[16,1,6,6,130]{4,0,3,2,1:T(8,128)(2,1)S(1)} %pad_bitcast_fusion) | data formatting | bytes 299520 | tf_op jit(solution)/shard_map/broadcast_in_dim | solution.py:60
  61.3 16.7 %fusion.52 = f32[32,3,3,3,16]{0,4,3,2,1:T(8,128)} fusion(bf16[16,1,6,6,130]{0,1,4,3,2:T(2,128)(2,1)S(1)} %copy.84, bf16[32,1,4,4,128]{0,1,4,3,2:T(2,128)(2,1)} %copy.85), kind=kOutput, calls=%fused_computation.69 | convolution fusion | flops 56623104 | bytes 336128 | tf_op jit(solution)/shard_map/transpose | solution.py:67
  78.4 4.3 %collective-permute-start.6 = (bf16[32,6,1,128]{3,0,2,1:T(8,128)(2,1)S(1)}, bf16[32,6,1,128]{3,0,2,1:T(8,128)(2,1)S(1)}, u32[]{:S(2)}, u32[]{:S(2)}) collective-permute-start(bf16[32,6,1,128]{3,0,2,1:T(8,128)(2,1)S(1)} %get-tuple-element.22), channel_id=1, source_target_pairs={{0,1},{1,2},{2,3},{3,4},{4,5},{5,6},{6,7},{7,8},{8,9},{9,10},{10,1... | collective-permute-start | bytes 147464 | tf_op jit(solution)/shard_map/ppermute | solution.py:14
  82.7 1.9 collective-permute-start.7
  85.4 0.7 copy.88
  86.1 119.2 %all-reduce.1 = (f32[32,27,16]{0,2,1:T(8,128)}, f32[32]{0:T(128)}) all-reduce(f32[32,27,16]{0,2,1:T(8,128)S(1)} %bitcast.106, f32[32]{0:T(128)S(1)} %convert_reduce_fusion), channel_id=1, replica_groups=mesh['block'=48,'chan'=16] {'block','chan'}, use_global_device_ids=true, to_apply=%region_1.2 | all-reduce | flops 13856 | bytes 110848 | tf_op jit(solution)/shard_map/psum | solution.py:69
  205.6 1.7 reshape.107
  207.4 3.0 %copy.80 = bf16[32,6,6,1,8,17]{0,4,5,2,1,3:T(8,128)(2,1)} copy(bf16[32,6,6,1,8,17]{5,4,0,2,1,3:T(8,128)(2,1)S(1)} %reshape.107) | data formatting | bytes 626688 | tf_op jit(solution)/shard_map/conv_general_dilated | solution.py:21
  210.4 1.0 slice.45
  211.4 3.2 %fusion.4 = bf16[4,4,8,17,16]{4,2,3,1,0:T(8,128)(2,1)S(1)} fusion(bf16[32,3,3,3,16]{0,4,3,2,1:T(8,128)(2,1)S(1)} %bitcast.95, bf16[32,6,6,1,7,2]{0,4,5,2,1,3:T(8,128)(2,1)S(1)} %slice.45, bf16[32,6,6,1,8,17]{0,4,5,2,1,3:T(8,128)(2,1)} %copy.80), kind=kOutput, calls=%fused_computation.7 | convolution fusion | flops 61212672 | bytes 442880 | tf_op jit(solution)/shard_map/conv_general_dilated | solution.py:21
  214.6 0.9 copy.81
  216.1 0.7 copy.89
  (55 shorter events, 4.4 us)
Async XLA Ops:
  0.6 41.4 %copy-start = (bf16[32,27,16]{0,2,1:T(8,128)(2,1)S(1)}, bf16[32,27,16]{0,2,1:T(8,128)(2,1)}, u32[]{:S(2)}) copy-start(bf16[32,27,16]{0,2,1:T(8,128)(2,1)} %param.5) | copy-start | bytes 82948
  1.4 7.0 %collective-permute-start = (bf16[16,1,4,128]{3,0,2,1:T(8,128)(2,1)S(1)}, bf16[16,1,4,128]{3,0,2,1:T(8,128)(2,1)S(1)}, u32[]{:S(2)}, u32[]{:S(2)}) collective-permute-start(bf16[16,1,4,128]{3,0,2,1:T(8,128)(2,1)S(1)} %copy.97), channel_id=1, source_target_pairs={{0,16},{16,32},{32,48},{48,64},{64,80},{80,96},{96,112},{112,128},... | collective-permute-start | bytes 49160 | tf_op jit(solution)/shard_map/ppermute | solution.py:14
  6.3 5.1 %collective-permute-start.1 = (bf16[16,1,4,128]{3,0,2,1:T(8,128)(2,1)S(1)}, bf16[16,1,4,128]{3,0,2,1:T(8,128)(2,1)S(1)}, u32[]{:S(2)}, u32[]{:S(2)}) collective-permute-start(bf16[16,1,4,128]{3,0,2,1:T(8,128)(2,1)S(1)} %copy.98), channel_id=1, source_target_pairs={{16,0},{32,16},{48,32},{64,48},{80,64},{96,80},{112,96},{128,112},... | collective-permute-start | bytes 49160 | tf_op jit(solution)/shard_map/ppermute | solution.py:15
  11.4 20.8 %collective-permute-start.2 = (bf16[16,6,1,128]{3,0,2,1:T(8,128)(2,1)S(1)}, bf16[16,6,1,128]{3,0,2,1:T(8,128)(2,1)S(1)}, u32[]{:S(2)}, u32[]{:S(2)}) collective-permute-start(bf16[16,6,1,128]{3,0,2,1:T(8,128)(2,1)S(1)} %get-tuple-element.28), channel_id=1, source_target_pairs={{0,1},{1,2},{2,3},{3,4},{4,5},{5,6},{6,7},{7,8},{8,9},{9,10},{10,1... | collective-permute-start | bytes 73736 | tf_op jit(solution)/shard_map/ppermute | solution.py:14
  27.4 11.5 %collective-permute-start.3 = (bf16[16,6,1,128]{3,0,2,1:T(8,128)(2,1)S(1)}, bf16[16,6,1,128]{3,0,2,1:T(8,128)(2,1)S(1)}, u32[]{:S(2)}, u32[]{:S(2)}) collective-permute-start(bf16[16,6,1,128]{3,0,2,1:T(8,128)(2,1)S(1)} %get-tuple-element.29), channel_id=1, source_target_pairs={{1,0},{2,1},{3,2},{4,3},{5,4},{6,5},{7,6},{8,7},{9,8},{10,9},{11,1... | collective-permute-start | bytes 73736 | tf_op jit(solution)/shard_map/ppermute | solution.py:15
  39.9 2.1 copy-start.6
  39.9 2.1 copy-start.8
  45.7 1.0 copy-start.3
  45.7 1.1 copy-start.2
  51.6 26.8 %collective-permute-start.4 = (bf16[32,1,4,128]{3,0,2,1:T(8,128)(2,1)}, bf16[32,1,4,128]{3,0,2,1:T(8,128)(2,1)S(1)}, u32[]{:S(2)}, u32[]{:S(2)}) collective-permute-start(bf16[32,1,4,128]{3,0,2,1:T(8,128)(2,1)} %get-tuple-element.26), channel_id=1, source_target_pairs={{0,16},{16,32},{32,48},{48,64},{64,80},{80,96},{96,112},{112,128},... | collective-permute-start | bytes 98312 | tf_op jit(solution)/shard_map/ppermute | solution.py:14
  55.3 23.1 %collective-permute-start.5 = (bf16[32,1,4,128]{3,0,2,1:T(8,128)(2,1)S(1)}, bf16[32,1,4,128]{3,0,2,1:T(8,128)(2,1)S(1)}, u32[]{:S(2)}, u32[]{:S(2)}) collective-permute-start(bf16[32,1,4,128]{3,0,2,1:T(8,128)(2,1)S(1)} %get-tuple-element.27), channel_id=1, source_target_pairs={{16,0},{32,16},{48,32},{64,48},{80,64},{96,80},{112,96},{128,112},... | collective-permute-start | bytes 98312 | tf_op jit(solution)/shard_map/ppermute | solution.py:15
  61.3 16.7 %copy-start.4 = (f32[32,2,2,64]{0,3,2,1:T(8,128)S(1)}, f32[32,2,2,64]{0,3,2,1:T(8,128)}, u32[]{:S(2)}) copy-start(f32[32,2,2,64]{0,3,2,1:T(8,128)} %fusion.23) | copy-start | bytes 98308
  61.3 16.8 %copy-start.1 = (f32[4,4,8,17,32]{4,2,3,1,0:T(8,128)S(1)}, f32[4,4,8,17,32]{4,2,3,1,0:T(8,128)}, u32[]{:S(2)}) copy-start(f32[4,4,8,17,32]{4,2,3,1,0:T(8,128)} %get-tuple-element.32) | copy-start | bytes 835588
  78.4 126.9 %collective-permute-start.6 = (bf16[32,6,1,128]{3,0,2,1:T(8,128)(2,1)S(1)}, bf16[32,6,1,128]{3,0,2,1:T(8,128)(2,1)S(1)}, u32[]{:S(2)}, u32[]{:S(2)}) collective-permute-start(bf16[32,6,1,128]{3,0,2,1:T(8,128)(2,1)S(1)} %get-tuple-element.22), channel_id=1, source_target_pairs={{0,1},{1,2},{2,3},{3,4},{4,5},{5,6},{6,7},{7,8},{8,9},{9,10},{10,1... | collective-permute-start | bytes 147464 | tf_op jit(solution)/shard_map/ppermute | solution.py:14
  82.7 122.6 %collective-permute-start.7 = (bf16[32,6,1,128]{3,0,2,1:T(8,128)(2,1)S(1)}, bf16[32,6,1,128]{3,0,2,1:T(8,128)(2,1)S(1)}, u32[]{:S(2)}, u32[]{:S(2)}) collective-permute-start(bf16[32,6,1,128]{3,0,2,1:T(8,128)(2,1)S(1)} %get-tuple-element.23), channel_id=1, source_target_pairs={{1,0},{2,1},{3,2},{4,3},{5,4},{6,5},{7,6},{8,7},{9,8},{10,9},{11,1... | collective-permute-start | bytes 147464 | tf_op jit(solution)/shard_map/ppermute | solution.py:15
  84.7 1.3 copy-start.5
  211.3 4.1 %copy-start.7 = (pred[8,17]{1,0:T(8,128)(4,1)S(1)}, pred[8,17]{1,0:T(8,128)(4,1)}, u32[]{:S(2)}) copy-start(pred[8,17]{1,0:T(8,128)(4,1)} %constant.29) | copy-start | bytes 412
where the time goes:
time: 220 us; the launch traced here: 217 us
  blocking collectives  119 us (54%)
  starting transfers between devices  35.1 us (16%)
  local copies, waits for them, and re-layouts  24.6 us (11%)
  matrix products  23 us (10%)
  waiting for transfers between devices  8.66 us (4%)
  other arithmetic  5.17 us (2%)
    psum x1, blocking collectives, local(): lax.psum((local_kernel, local_bias), ('block', 'chan'))  119 us
    ppermute x4, starting transfers between devices, extended(): before = lax.ppermute(last, axis, up)  28.7 us
    transpose x1, matrix products, local(): local_kernel.transpose(1, 2, 3, 4, 0).reshape(out_chan, 27, in_chan)  16.7 us
    conv_general_dilated x10, local copies, waits for them, and re-layouts, conv_valid(): lax.conv_general_dilated(inputs[None], filters, (1, 1, 1), ((0, 0), (0, 0...  10 us
    ppermute x4, waiting for transfers between devices, extended(): after = lax.ppermute(initial, axis, down)  8.65 us
    ppermute x4, starting transfers between devices, extended(): after = lax.ppermute(initial, axis, down)  6.43 us
    conv_general_dilated x2, matrix products, conv_valid(): lax.conv_general_dilated(inputs[None], filters, (1, 1, 1), ((0, 0), (0, 0...  6.25 us
    unnamed x27, local copies, waits for them, and re-layouts  4.47 us
  transfers between devices with their start and end apart: 8, of which 2 were waited for; matrix products, arithmetic and copies ran while one was open for 13% of the time, Pallas kernels for 0%

commit v1 on v0

v1 whole, which is shorter than its diff:
```python
import functools

import jax
import jax.numpy as jnp
from jax import lax
from jax.experimental import pallas as pl
from jax.experimental.pallas import tpu as pltpu
from jax.sharding import PartitionSpec as P

MESH = pl.DeviceIdType.MESH
F32 = jnp.float32
BF16 = jnp.bfloat16
DIRECTIONS = [(i, j) for i in (-1, 0, 1) for j in (-1, 0, 1) if (i, j) != (0, 0)]


def span_out(step):
    return slice(1, 5) if step == 0 else (slice(4, 5) if step > 0 else slice(1, 2))


def span_in(step):
    return slice(1, 5) if step == 0 else (slice(0, 1) if step > 0 else slice(5, 6))


def nt_dot(a, b):
    return lax.dot_general(a, b, (((1,), (1,)), ((), ())), preferred_element_type=F32)


def kernel(factors, vt, w_fwd, w_back, bias, coarse, pooled_o, vgrad_o, kgrad_o,
           wide, shifted, cols, pre, grad, cols_back, terms, from_one, from_two, from_three, result,
           halo_send, halo_recv, grad_send, grad_recv, one_send, one_recv, two_send, two_recv,
           three_send, three_recv, four_send, four_recv):
    ny, nzl, nx, nzh, ncore = factors
    nblock, nchan = ny * nzl, nx * nzh * ncore
    blk, chn = lax.axis_index("block"), lax.axis_index("chan")
    y, zl = lax.div(blk, nzl), lax.rem(blk, nzl)
    x, zh, core = lax.div(chn, nzh * ncore), lax.rem(lax.div(chn, ncore), nzh), lax.rem(chn, ncore)
    n_one, n_two, n_three = nx * ncore, ny, nzh * nzl
    me_one, me_two, me_three = x * ncore + core, y, zh * nzl + zl

    def dev_one(k):
        return (blk, lax.div(k, ncore) * (nzh * ncore) + zh * ncore + lax.rem(k, ncore))

    def dev_two(k):
        return (k * nzl + zl, chn)

    def dev_three(k):
        return (y * nzl + lax.rem(k, nzl), x * (nzh * ncore) + lax.div(k, nzl) * ncore + core)

    def inside(di, dj):
        ok = (blk + di >= 0) & (blk + di < nblock) & (chn + dj >= 0) & (chn + dj < nchan)
        return ok

    groups = ((n_one, me_one, dev_one), (n_two, me_two, dev_two), (n_three, me_three, dev_three))

    wide[...] = jnp.zeros_like(wide)
    grad[...] = jnp.zeros_like(grad)

    barrier = pltpu.get_barrier_semaphore()
    count = jnp.int32(n_one + n_two + n_three - 3)
    for di, dj in DIRECTIONS:
        ok = inside(di, dj)
        count = count + ok.astype(jnp.int32)

        @pl.when(ok)
        def _(di=di, dj=dj):
            pl.semaphore_signal(barrier, inc=1, device_id=(blk + di, chn + dj), device_id_type=MESH)
    for n, me, dev in groups:
        for k in range(1, n):
            pl.semaphore_signal(barrier, inc=1, device_id=dev(lax.rem(me + k, n)), device_id_type=MESH)
    wide[1:5, 1:5] = vt[...]
    cols[:, :, 432:512, :] = jnp.ones((4, 4, 80, 128), BF16)
    pl.semaphore_wait(barrier, count)

    def halo(buf, send, recv, which):
        di, dj = DIRECTIONS[which]
        return pltpu.make_async_remote_copy(
            src_ref=buf.at[span_out(di), span_out(dj)],
            dst_ref=buf.at[span_in(di), span_in(dj)],
            send_sem=send.at[which], recv_sem=recv.at[which],
            device_id=(blk + di, chn + dj), device_id_type=MESH)

    def halo_start(buf, send, recv):
        for which, (di, dj) in enumerate(DIRECTIONS):
            @pl.when(inside(di, dj))
            def _(which=which):
                halo(buf, send, recv, which).start()

    def halo_recv_wait(buf, send, recv):
        for which, (di, dj) in enumerate(DIRECTIONS):
            @pl.when(inside(-di, -dj))
            def _(which=which):
                halo(buf, send, recv, which).wait_recv()

    def halo_send_wait(buf, send, recv):
        for which, (di, dj) in enumerate(DIRECTIONS):
            @pl.when(inside(di, dj))
            def _(which=which):
                halo(buf, send, recv, which).wait_send()

    def group_copy(stage, k, src, dst, send, recv):
        n, me, dev = groups[stage]
        return pltpu.make_async_remote_copy(
            src_ref=src, dst_ref=dst, send_sem=send.at[k], recv_sem=recv.at[k],
            device_id=dev(lax.rem(me + k, n)), device_id_type=MESH)

    halo_start(wide, halo_send, halo_recv)

    row = lax.broadcasted_iota(jnp.int32, (64, 128), 0)
    lane = lax.broadcasted_iota(jnp.int32, (64, 128), 1)
    up_map = (lax.shift_right_logical(lane, 1) == row).astype(F32).astype(BF16)
    ups = [[jnp.dot(coarse[i, j], up_map, preferred_element_type=F32) * 0.125 for j in range(2)] for i in range(2)]
    row2 = lax.broadcasted_iota(jnp.int32, (128, 256), 0)
    lane2 = lax.broadcasted_iota(jnp.int32, (128, 256), 1)
    shift_map = (row2 == jnp.where(lane2 < 128, lane2 - 1, lane2 - 127)).astype(F32).astype(BF16)

    halo_recv_wait(wide, halo_send, halo_recv)

    for i in range(6):
        moved = jnp.dot(wide[i].reshape(96, 128), shift_map, preferred_element_type=F32).astype(BF16)
        shifted[0, i] = moved[:, :128].reshape(6, 16, 128)
        shifted[1, i] = moved[:, 128:].reshape(6, 16, 128)
    for a in range(3):
        for b in range(3):
            for d in range(3):
                t = 9 * a + 3 * b + d
                source = wide if d == 1 else shifted.at[d // 2]
                cols[:, :, 16 * t:16 * t + 16, :] = source[a:a + 4, b:b + 4]
    kacc = jnp.zeros((32, 512), F32)
    for i in range(4):
        for j in range(4):
            act = jnp.dot(w_fwd[...], cols[i, j], preferred_element_type=F32) + bias[...]
            pre[i, j] = act
            slope = 0.2 + 0.8 * jax.nn.sigmoid(act)
            grad[1 + i, 1 + j] = (ups[i // 2][j // 2] * slope).astype(BF16)
    halo_start(grad, grad_send, grad_recv)
    for i in range(4):
        for j in range(0, 4, 2):
            left = jnp.concatenate([grad[1 + i, 1 + j], grad[1 + i, 2 + j]], axis=1)
            right = jnp.concatenate([cols[i, j], cols[i, j + 1]], axis=1)
            kacc = kacc + nt_dot(left, right)
    for s in range(16):
        r, l = s // 4, s % 4
        terms[s] = kacc[8 * r:8 * r + 8, 128 * l:128 * l + 128]

    per = 16 // n_one
    own = pl.ds(me_one * per, per)
    copies = []

    def send_all(stage, make):
        started = [make(k) for k in range(1, groups[stage][0])]
        for c in started:
            c.start()
        copies.extend(started)
        return started

    def total(buf, n):
        acc = buf[0]
        for k in range(1, n):
            acc = acc + buf[k]
        return acc

    one = send_all(0, lambda k: group_copy(
        0, k, terms.at[pl.ds(lax.rem(me_one + k, n_one) * per, per)], from_one.at[me_one], one_send, one_recv))
    from_one[me_one] = terms[own]

    pool_row = lax.broadcasted_iota(jnp.int32, (128, 64), 0)
    pool_lane = lax.broadcasted_iota(jnp.int32, (128, 64), 1)
    pool_map = jnp.where(lax.shift_right_logical(pool_row, 1) == pool_lane, 0.125, 0.0).astype(F32)
    for i in range(2):
        for j in range(2):
            acc = None
            for p in range(2):
                for q in range(2):
                    v = pre[2 * i + p, 2 * j + q]
                    smooth = 0.2 * v + 0.8 * (jnp.maximum(v, 0.0) + jnp.log1p(jnp.exp(-jnp.abs(v))))
                    acc = smooth if acc is None else acc + smooth
            pooled_o[i, j] = jnp.dot(acc, pool_map, precision=lax.Precision.HIGHEST,
                                     preferred_element_type=F32).astype(BF16)

    for c in one:
        c.wait_recv()
    from_two[me_two] = total(from_one, n_one)
    two = send_all(1, lambda k: group_copy(1, k, from_two.at[me_two], from_two.at[me_two], two_send, two_recv))

    halo_recv_wait(grad, grad_send, grad_recv)
    for a in range(3):
        for b in range(3):
            t = 3 * a + b
            cols_back[:, :, 32 * t:32 * t + 32, :] = grad[a:a + 4, b:b + 4]
    zlane = lax.broadcasted_iota(jnp.int32, (16, 128), 1)

    def back_row(i):
        for j in range(4):
            part = jnp.dot(w_back[...], cols_back[i, j], preferred_element_type=F32)
            before = jnp.where(zlane == 0, 0.0, pltpu.roll(part[:16], 1, 1))
            after = jnp.where(zlane == 127, 0.0, pltpu.roll(part[32:], 127, 1))
            vgrad_o[i, j] = (before + part[16:32] + after).astype(BF16)

    for c in two:
        c.wait_recv()
    from_three[me_three] = total(from_two, n_two)
    three = send_all(2, lambda k: group_copy(2, k, from_three.at[me_three], from_three.at[me_three], three_send, three_recv))
    back_row(0)
    back_row(1)
    for c in three:
        c.wait_recv()
    result[own] = total(from_three, n_three)
    four = send_all(0, lambda k: group_copy(0, k, result.at[own], result.at[own], four_send, four_recv))
    back_row(2)
    back_row(3)
    halo_send_wait(wide, halo_send, halo_recv)
    halo_send_wait(grad, grad_send, grad_recv)
    for c in four:
        c.wait_recv()
    for s in range(16):
        r, l = s // 4, s % 4
        kgrad_o[8 * r:8 * r + 8, 128 * l:128 * l + 128] = result[s]
    for c in copies:
        c.wait_send()


def factors_of(mesh):
    nblock, nchan = mesh.shape["block"], mesh.shape["chan"]
    if (nblock, nchan) == (48, 16):
        return (8, 6, 4, 2, 2)
    return (2, nblock // 2, nchan // 4, 2, 2)


def local(factors, volume, weights, conv_bias, pooled_grad):
    ny, nzl, nx, nzh, ncore = factors
    n_one, n_two, n_three = nx * ncore, ny, nzh * nzl
    per = 16 // n_one
    vt = volume.transpose(1, 2, 0, 3)
    w_fwd = jnp.pad(weights.reshape(32, 432), ((0, 0), (0, 80)))
    w5 = weights.reshape(32, 3, 3, 3, 16)[:, ::-1, ::-1, ::-1, :]
    w_back = w5.transpose(3, 4, 1, 2, 0).reshape(48, 288)
    coarse = pooled_grad.transpose(1, 2, 0, 3)
    vmem = pl.BlockSpec(memory_space=pltpu.VMEM)
    dma = pltpu.SemaphoreType.DMA
    pooled, vgrad, kgrad = pl.pallas_call(
        functools.partial(kernel, factors),
        out_shape=(jax.ShapeDtypeStruct((2, 2, 32, 64), BF16),
                   jax.ShapeDtypeStruct((4, 4, 16, 128), BF16),
                   jax.ShapeDtypeStruct((32, 512), F32)),
        in_specs=[vmem] * 5,
        out_specs=(vmem, vmem, vmem),
        scratch_shapes=[
            pltpu.VMEM((6, 6, 16, 128), BF16),
            pltpu.VMEM((2, 6, 6, 16, 128), BF16),
            pltpu.VMEM((4, 4, 512, 128), BF16),
            pltpu.VMEM((4, 4, 32, 128), F32),
            pltpu.VMEM((6, 6, 32, 128), BF16),
            pltpu.VMEM((4, 4, 288, 128), BF16),
            pltpu.VMEM((16, 8, 128), F32),
            pltpu.VMEM((n_one, per, 8, 128), F32),
            pltpu.VMEM((n_two, per, 8, 128), F32),
            pltpu.VMEM((n_three, per, 8, 128), F32),
            pltpu.VMEM((16, 8, 128), F32),
            dma((8,)), dma((8,)), dma((8,)), dma((8,)),
            dma((n_one,)), dma((n_one,)), dma((n_two,)), dma((n_two,)),
            dma((n_three,)), dma((n_three,)), dma((n_one,)), dma((n_one,)),
        ],
        compiler_params=pltpu.CompilerParams(
            collective_id=0, has_side_effects=True, vmem_limit_bytes=32 * 1024 * 1024),
        name="conv_step",
    )(vt, w_fwd, w_back, conv_bias[:, None], coarse)
    return (pooled.transpose(2, 0, 1, 3), vgrad.transpose(2, 0, 1, 3),
            kgrad[:, :432].reshape(32, 27, 16), kgrad[:, 432])


def solution(mesh):
    placed = (P(None, "block", "chan", None), P(), P(), P(None, "block", "chan", None))
    return jax.shard_map(
        functools.partial(local, factors_of(mesh)),
        mesh=mesh,
        in_specs=placed,
        out_specs=(P(None, "block", "chan", None), P(None, "block", "chan", None), P(), P()),
        check_vma=False,
    )
```

time: 220 us -> 56.4 us (0.26); the launches traced: 217 us -> 56.1 us
  blocking collectives: 119 us -> 0 us
  Pallas kernels: 0 us -> 47.9 us
  starting transfers between devices: 35.1 us -> 0 us
  matrix products: 23 us -> 0 us
  local copies, waits for them, and re-layouts: 24.6 us -> 7.54 us
  waiting for transfers between devices: 8.66 us -> 0 us
  other arithmetic: 5.17 us -> 0 us
    psum x1 -> x0, blocking collectives: 119 us -> none  [local(): lax.psum((local_kernel, local_bias), ('block', 'chan'))]
    pallas_call x0 -> x1, Pallas kernels: none -> 47.9 us  [local(): pl.pallas_call(functools.partial(kernel, factors), out_shape=(jax.ShapeDt...]
    ppermute x8 -> x0, starting transfers between devices: 35.1 us -> none  [the longest x4 28.7 us: extended(): before = lax.ppermute(last, axis, up)]
    transpose x1 -> x0, matrix products: 16.7 us -> none  [local(): local_kernel.transpose(1, 2, 3, 4, 0).reshape(out_chan, 27, in_chan)]
    conv_general_dilated x10 -> x0, local copies, waits for them, and re-layouts: 10 us -> none  [conv_valid(): lax.conv_general_dilated(inputs[None], filters, (1, 1, 1), ((0, 0), (0, 0...]
    ppermute x8 -> x0, waiting for transfers between devices: 8.66 us -> none  [the longest x4 8.65 us: extended(): after = lax.ppermute(initial, axis, down)]
    conv_general_dilated x2 -> x0, matrix products: 6.25 us -> none  [conv_valid(): lax.conv_general_dilated(inputs[None], filters, (1, 1, 1), ((0, 0), (0, 0...]
    reduce_sum x2 -> x0, other arithmetic: 4.55 us -> none  [the longest x1 3.95 us: local(): pooled = smooth.reshape(out_chan, row_count // 2, 2, col_count // 2, 2, d...]
  transfers between devices with their start and end apart: 8 -> 0, of which waited for: 2 -> 0; matrix products, arithmetic and copies ran while one was open for 13% -> 0% of each run, Pallas kernels for 0% -> 0%
where the time goes in v1:
time: 56.4 us; the launch traced here: 56.1 us
  Pallas kernels  47.9 us (85%)
  local copies, waits for them, and re-layouts  7.54 us (13%)
  between operations  0.69 us (1%)
    pallas_call x1, Pallas kernels, local(): pl.pallas_call(functools.partial(kernel, factors), out_shape=(jax.ShapeDt...  47.9 us
    unnamed x12, local copies, waits for them, and re-layouts  4.29 us

profile of v1, /device:TPU:1, one launch (start us, length us, event | category | flops | bytes accessed | tf_op | source)
XLA Modules:
  0.0 56.1 jit_solution(11615073661838305774)
XLA Ops:
  0.6 1.0 %copy.18 = bf16[32,3,3,3,16]{0,2,1,4,3:T(4,128)(2,1)S(1)} copy(bf16[32,3,3,3,16]{0,4,3,2,1:T(8,128)(2,1)} %bitcast.20) | data formatting | bytes 55296 | tf_op jit(solution)/shard_map/reshape | solution.py:235
  1.6 0.5 rev.3
  2.1 0.0 copy-start.1
  2.1 0.1 reshape.22.w_back
  2.2 0.7 %copy-done.1 = bf16[16,4,4,128]{3,2,1,0:T(4,128)(2,1)S(1)} copy-done((bf16[16,4,4,128]{3,2,1,0:T(4,128)(2,1)S(1)}, bf16[16,4,4,128]{3,2,1,0:T(4,128)(2,1)}, u32[]{:S(2)}) %copy-start.1) | copy-done | bytes 65560
  2.9 0.0 copy-start
  2.9 0.9 %copy-done = bf16[32,27,16]{0,2,1:T(8,128)(2,1)S(1)} copy-done((bf16[32,27,16]{0,2,1:T(8,128)(2,1)S(1)}, bf16[32,27,16]{0,2,1:T(8,128)(2,1)}, u32[]{:S(2)}) %copy-start) | copy-done | bytes 27672
  3.8 0.1 copy.17
  3.9 0.0 copy-start.2
  3.9 0.7 %copy-done.2 = bf16[32,2,2,64]{3,2,1,0:T(2,128)(2,1)S(1)} copy-done((bf16[32,2,2,64]{3,2,1,0:T(2,128)(2,1)S(1)}, bf16[32,2,2,64]{3,2,1,0:T(2,128)(2,1)}, u32[]{:S(2)}) %copy-start.2) | copy-done | bytes 16408
  4.7 0.0 copy-start.3
  4.7 0.6 %copy-done.3 = f32[32]{0:T(128)S(1)} copy-done((f32[32]{0:T(128)S(1)}, f32[32]{0:T(128)}, u32[]{:S(2)}) %copy-start.3) | copy-done | bytes 152
  5.3 0.1 copy.20.bias
  5.4 47.9 %conv_step.1 = (bf16[2,2,32,64]{3,2,1,0:T(8,128)(2,1)S(1)}, bf16[4,4,16,128]{3,2,1,0:T(8,128)(2,1)S(1)}, f32[32,512]{1,0:T(8,128)S(1)}) custom-call(bf16[4,4,16,128]{3,2,1,0:T(8,128)(2,1)S(1)} %bitcast.14, bf16[32,512]{1,0:T(8,128)(2,1)S(1)} %pad.4.w_fwd, bf16[48,288]{1,0:T(8,128)(2,1)S(1)} %reshape.22.w_back, f32[32,1]{1,0:T(8,128)S(1)} %copy.20.bias, ...), custom_call_target="tpu_custom_call" | custom-call | tf_op jit(solution)/shard_map/conv_step/pallas_call | solution.py:240
  53.3 0.8 %copy.21 = f32[32,432]{0,1:T(8,128)} copy(f32[32,432]{1,0:T(8,128)S(1)} %bitcast.16) | data formatting | bytes 110592 | tf_op jit(solution)/shard_map/slice | solution.py:268
  54.1 0.7 %slice_reduce_fusion = f32[32]{0:T(128)} fusion(f32[32,512]{1,0:T(8,128)S(1)} %get-tuple-element.9), kind=kLoop, calls=%fused_computation.2 | loop fusion | bytes 256 | tf_op jit(solution)/shard_map/slice | solution.py:268
  54.8 0.7 %copy.23 = bf16[16,4,4,128]{3,2,1,0:T(4,128)(2,1)} copy(bf16[16,4,4,128]{3,0,2,1:T(8,128)(2,1)S(1)} %bitcast.17) | data formatting | bytes 131072
  55.5 0.6 %copy.22 = bf16[32,2,2,64]{3,2,1,0:T(2,128)(2,1)} copy(bf16[32,2,2,64]{3,0,2,1:T(8,128)(2,1)S(1)} %bitcast.18) | data formatting | bytes 32768
  (3 shorter events, 0.0 us)
Async XLA Ops:
  2.1 0.8 %copy-start.1 = (bf16[16,4,4,128]{3,2,1,0:T(4,128)(2,1)S(1)}, bf16[16,4,4,128]{3,2,1,0:T(4,128)(2,1)}, u32[]{:S(2)}) copy-start(bf16[16,4,4,128]{3,2,1,0:T(4,128)(2,1)} %param.4) | copy-start | bytes 196612
  2.9 0.9 %copy-start = (bf16[32,27,16]{0,2,1:T(8,128)(2,1)S(1)}, bf16[32,27,16]{0,2,1:T(8,128)(2,1)}, u32[]{:S(2)}) copy-start(bf16[32,27,16]{0,2,1:T(8,128)(2,1)} %param.5) | copy-start | bytes 82948
  3.9 0.8 %copy-start.2 = (bf16[32,2,2,64]{3,2,1,0:T(2,128)(2,1)S(1)}, bf16[32,2,2,64]{3,2,1,0:T(2,128)(2,1)}, u32[]{:S(2)}) copy-start(bf16[32,2,2,64]{3,2,1,0:T(2,128)(2,1)} %param.7) | copy-start | bytes 49156
  4.7 0.7 %copy-start.3 = (f32[32]{0:T(128)S(1)}, f32[32]{0:T(128)}, u32[]{:S(2)}) copy-start(f32[32]{0:T(128)} %param.6) | copy-start | bytes 388

commit v2 on v1

v2 whole, which is shorter than its diff:
```python
import functools

import jax
import jax.numpy as jnp
from jax import lax
from jax.experimental import pallas as pl
from jax.experimental.pallas import tpu as pltpu
from jax.sharding import PartitionSpec as P

MESH = pl.DeviceIdType.MESH
F32 = jnp.float32
BF16 = jnp.bfloat16
DIRECTIONS = [(i, j) for j in (-1, 1, 0) for i in (-1, 1, 0) if (i, j) != (0, 0)]


def span_out(step):
    return slice(1, 5) if step == 0 else (slice(4, 5) if step > 0 else slice(1, 2))


def span_in(step):
    return slice(1, 5) if step == 0 else (slice(0, 1) if step > 0 else slice(5, 6))


def nt_dot(a, b):
    return lax.dot_general(a, b, (((1,), (1,)), ((), ())), preferred_element_type=F32)


def far_first(n):
    return sorted(range(1, n), key=lambda k: -min(k, n - k))


def kernel(factors, volume_h, weights_h, bias_h, coarse_h, pooled_o, vgrad_o, kgrad_o, bgrad_o,
           volume_v, weights_v, bias_v, coarse_v, vol_f, coarse_f, pool_f,
           wide, shifted, cols, pre, grad, cols_back, w_back, terms, from_one, from_two, from_three, result,
           in_sem, halo_send, halo_recv, grad_send, grad_recv, stage_send, stage_recv):
    ny, nzl, nx, nzh, ncore = factors
    nblock, nchan = ny * nzl, nx * nzh * ncore
    blk, chn = lax.axis_index("block"), lax.axis_index("chan")
    y, zl = lax.div(blk, nzl), lax.rem(blk, nzl)
    x, zh, core = lax.div(chn, nzh * ncore), lax.rem(lax.div(chn, ncore), nzh), lax.rem(chn, ncore)
    n_one, n_two, n_three = nx * ncore, ny, nzh * nzl
    me_one, me_two, me_three = x * ncore + core, y, zh * nzl + zl

    def dev_one(k):
        return (blk, lax.div(k, ncore) * (nzh * ncore) + zh * ncore + lax.rem(k, ncore))

    def dev_two(k):
        return (k * nzl + zl, chn)

    def dev_three(k):
        return (y * nzl + lax.rem(k, nzl), x * (nzh * ncore) + lax.div(k, nzl) * ncore + core)

    def inside(di, dj):
        return (blk + di >= 0) & (blk + di < nblock) & (chn + dj >= 0) & (chn + dj < nchan)

    groups = ((n_one, me_one, dev_one), (n_two, me_two, dev_two), (n_three, me_three, dev_three))

    barrier = pltpu.get_barrier_semaphore()
    count = jnp.int32(n_one + n_two + n_three - 3)
    for di, dj in DIRECTIONS:
        ok = inside(di, dj)
        count = count + ok.astype(jnp.int32)

        @pl.when(ok)
        def _(di=di, dj=dj):
            pl.semaphore_signal(barrier, inc=1, device_id=(blk + di, chn + dj), device_id_type=MESH)
    loads = [pltpu.make_async_copy(src, dst, in_sem.at[i]) for i, (src, dst) in enumerate(
        ((volume_h, volume_v), (weights_h, weights_v), (bias_h, bias_v), (coarse_h, coarse_v)))]
    for load in loads:
        load.start()
    for n, me, dev in groups:
        for k in far_first(n):
            pl.semaphore_signal(barrier, inc=1, device_id=dev(lax.rem(me + k, n)), device_id_type=MESH)
    loads[0].wait()
    vol_f[...] = volume_v[...].astype(F32)
    for i in range(4):
        for j in range(4):
            wide[1 + i, 1 + j] = vol_f[:, i, j, :].astype(BF16)
    pl.semaphore_wait(barrier, count)

    def halo(buf, send, recv, which):
        di, dj = DIRECTIONS[which]
        return pltpu.make_async_remote_copy(
            src_ref=buf.at[span_out(di), span_out(dj)],
            dst_ref=buf.at[span_in(di), span_in(dj)],
            send_sem=send.at[which], recv_sem=recv.at[which],
            device_id=(blk + di, chn + dj), device_id_type=MESH)

    def halo_start(buf, send, recv):
        for which, (di, dj) in enumerate(DIRECTIONS):
            @pl.when(inside(di, dj))
            def _(which=which):
                halo(buf, send, recv, which).start()

    def halo_recv_wait(buf, send, recv):
        for which, (di, dj) in enumerate(DIRECTIONS):
            @pl.when(inside(-di, -dj))
            def _(which=which):
                halo(buf, send, recv, which).wait_recv()

    def halo_send_wait(buf, send, recv):
        for which, (di, dj) in enumerate(DIRECTIONS):
            @pl.when(inside(di, dj))
            def _(which=which):
                halo(buf, send, recv, which).wait_send()

    def clear_rim(buf):
        for di, dj in DIRECTIONS:
            @pl.when(jnp.logical_not(inside(-di, -dj)))
            def _(di=di, dj=dj):
                part = (span_in(di), span_in(dj))
                buf[part] = jnp.zeros((part[0].stop - part[0].start, part[1].stop - part[1].start) + buf.shape[2:], BF16)

    halo_start(wide, halo_send, halo_recv)

    clear_rim(wide)
    clear_rim(grad)
    cols[:, :, 432:512, :] = jnp.ones((4, 4, 80, 128), BF16)
    for load in loads[1:]:
        load.wait()
    row = lax.broadcasted_iota(jnp.int32, (64, 128), 0)
    lane = lax.broadcasted_iota(jnp.int32, (64, 128), 1)
    up_map = (lax.shift_right_logical(lane, 1) == row).astype(F32).astype(BF16)
    coarse_f[...] = coarse_v[...].astype(F32)
    ups = [[jnp.dot(coarse_f[:, i, j, :].astype(BF16), up_map, preferred_element_type=F32) * 0.125
            for j in range(2)] for i in range(2)]
    row2 = lax.broadcasted_iota(jnp.int32, (128, 256), 0)
    lane2 = lax.broadcasted_iota(jnp.int32, (128, 256), 1)
    shift_map = (row2 == jnp.where(lane2 < 128, lane2 - 1, lane2 - 127)).astype(F32).astype(BF16)
    eye = (lax.broadcasted_iota(jnp.int32, (32, 32), 0) == lax.broadcasted_iota(jnp.int32, (32, 32), 1)).astype(F32)
    bias = jnp.sum(eye * bias_v[...], axis=1, keepdims=True)
    w_t = jnp.concatenate([weights_v[...].reshape(432, 32), jnp.zeros((80, 32), BF16)], axis=0)
    w_fwd = nt_dot(eye.astype(BF16), w_t).astype(BF16)
    for d in range(3):
        w_back[16 * d:16 * d + 16, :] = jnp.concatenate(
            [weights_v[26 - 3 * s - d] for s in range(9)], axis=1)

    halo_recv_wait(wide, halo_send, halo_recv)

    for i in range(6):
        moved = jnp.dot(wide[i].reshape(96, 128), shift_map, preferred_element_type=F32).astype(BF16)
        shifted[0, i] = moved[:, :128].reshape(6, 16, 128)
        shifted[1, i] = moved[:, 128:].reshape(6, 16, 128)
    for a in range(3):
        for b in range(3):
            for d in range(3):
                t = 9 * a + 3 * b + d
                source = wide if d == 1 else shifted.at[d // 2]
                cols[:, :, 16 * t:16 * t + 16, :] = source[a:a + 4, b:b + 4]
    for i in range(4):
        for j in range(4):
            act = jnp.dot(w_fwd, cols[i, j], preferred_element_type=F32) + bias
            pre[i, j] = act
            slope = 0.2 + 0.8 * jax.nn.sigmoid(act)
            grad[1 + i, 1 + j] = (ups[i // 2][j // 2] * slope).astype(BF16)
    kacc = jnp.zeros((128, 128), F32)
    for i in range(4):
        for j in range(0, 4, 2):
            pair = jnp.concatenate([grad[1 + i, 1 + j], grad[1 + i, 2 + j]], axis=1)
            for q in range(4):
                left = jnp.concatenate([cols[i, j, 128 * q:128 * q + 128, :],
                                        cols[i, j + 1, 128 * q:128 * q + 128, :]], axis=1)
                blocks = [jnp.zeros((32, 256), BF16)] * 4
                blocks[q] = pair
                kacc = kacc + nt_dot(left, jnp.concatenate(blocks, axis=0))
    terms[...] = kacc.reshape(16, 8, 128)

    per = 16 // n_one
    own = pl.ds(me_one * per, per)

    def stage_copy(stage, group, k, src, dst):
        n, me, dev = groups[group]
        return pltpu.make_async_remote_copy(
            src_ref=src, dst_ref=dst, send_sem=stage_send.at[stage], recv_sem=stage_recv.at[stage],
            device_id=dev(lax.rem(me + k, n)), device_id_type=MESH)

    def stage_all(stage, buf, n):
        ref = buf.at[pl.ds(0, n - 1)] if stage < 3 else buf.at[pl.ds(0, (n - 1) * per)]
        return pltpu.make_async_remote_copy(
            src_ref=ref, dst_ref=ref, send_sem=stage_send.at[stage], recv_sem=stage_recv.at[stage],
            device_id=(blk, chn), device_id_type=MESH)

    def total(buf, n):
        acc = buf[0]
        for k in range(1, n):
            acc = acc + buf[k]
        return acc

    for k in far_first(n_one):
        stage_copy(0, 0, k, terms.at[pl.ds(lax.rem(me_one + k, n_one) * per, per)], from_one.at[me_one]).start()
    from_one[me_one] = terms[own]
    halo_start(grad, grad_send, grad_recv)
    halo_send_wait(wide, halo_send, halo_recv)

    stage_all(0, from_one, n_one).wait_recv()
    from_two[me_two] = total(from_one, n_one)
    for k in far_first(n_two):
        stage_copy(1, 1, k, from_two.at[me_two], from_two.at[me_two]).start()

    pool_row = lax.broadcasted_iota(jnp.int32, (128, 64), 0)
    pool_lane = lax.broadcasted_iota(jnp.int32, (128, 64), 1)
    pool_map = jnp.where(lax.shift_right_logical(pool_row, 1) == pool_lane, 0.125, 0.0).astype(F32)
    for i in range(2):
        for j in range(2):
            acc = None
            for p in range(2):
                for q in range(2):
                    v = pre[2 * i + p, 2 * j + q]
                    smooth = 0.2 * v + 0.8 * (jnp.maximum(v, 0.0) + jnp.log1p(jnp.exp(-jnp.abs(v))))
                    acc = smooth if acc is None else acc + smooth
            pool_f[:, i, j, :] = jnp.dot(acc, pool_map, precision=lax.Precision.HIGHEST, preferred_element_type=F32)
    pooled_o[...] = pool_f[...].astype(BF16)
    stage_all(0, from_one, n_one).wait_send()

    stage_all(1, from_two, n_two).wait_recv()
    from_three[me_three] = total(from_two, n_two)
    for k in far_first(n_three):
        stage_copy(2, 2, k, from_three.at[me_three], from_three.at[me_three]).start()

    stage_all(1, from_two, n_two).wait_send()
    halo_recv_wait(grad, grad_send, grad_recv)
    for a in range(3):
        for b in range(3):
            t = 3 * a + b
            cols_back[:, :, 32 * t:32 * t + 32, :] = grad[a:a + 4, b:b + 4]
    zlane = lax.broadcasted_iota(jnp.int32, (16, 128), 1)
    for i in range(4):
        for j in range(4):
            part = jnp.dot(w_back[...], cols_back[i, j], preferred_element_type=F32)
            before = jnp.where(zlane == 0, 0.0, pltpu.roll(part[:16], 1, 1))
            after = jnp.where(zlane == 127, 0.0, pltpu.roll(part[32:], 127, 1))
            vol_f[:, i, j, :] = before + part[16:32] + after
    vgrad_o[...] = vol_f[...].astype(BF16)
    halo_send_wait(grad, grad_send, grad_recv)

    stage_all(2, from_three, n_three).wait_recv()
    result[own] = total(from_three, n_three)
    for k in far_first(n_one):
        stage_copy(3, 0, k, result.at[own], result.at[own]).start()
    stage_all(2, from_three, n_three).wait_send()
    stage_all(3, result, n_one).wait_recv()
    full = result[...].reshape(128, 128)
    for q in range(4):
        part = full if q == 0 else pltpu.roll(full, 128 - 32 * q, 1)
        taps = 8 if q < 3 else 3
        kgrad_o[8 * q:8 * q + taps] = part[:16 * taps, :32].reshape(taps, 16, 32)
    bgrad_o[...] = part[48:49, :32]
    stage_all(3, result, n_one).wait_send()


def leave(pooled_v, vgrad_v, kgrad_v, bgrad_v, pooled_h, vgrad_h, kgrad_h, bgrad_h, sem):
    copies = [pltpu.make_async_copy(src, dst, sem.at[i]) for i, (src, dst) in enumerate(
        ((vgrad_v, vgrad_h), (kgrad_v, kgrad_h), (pooled_v, pooled_h), (bgrad_v, bgrad_h)))]
    for c in copies:
        c.start()
    for c in copies:
        c.wait()


def factors_of(mesh):
    nblock, nchan = mesh.shape["block"], mesh.shape["chan"]
    if (nblock, nchan) == (48, 16):
        return (8, 6, 4, 2, 2)
    return (2, nblock // 2, nchan // 4, 2, 2)


def local(factors, volume, weights, conv_bias, pooled_grad):
    ny, nzl, nx, nzh, ncore = factors
    n_one, n_two, n_three = nx * ncore, ny, nzh * nzl
    per = 16 // n_one
    vmem = pl.BlockSpec(memory_space=pltpu.VMEM)
    hbm = pl.BlockSpec(memory_space=pltpu.HBM)
    dma = pltpu.SemaphoreType.DMA
    shapes = (jax.ShapeDtypeStruct((32, 2, 2, 64), BF16), jax.ShapeDtypeStruct((16, 4, 4, 128), BF16),
              jax.ShapeDtypeStruct((27, 16, 32), F32), jax.ShapeDtypeStruct((1, 32), F32))
    outs = pl.pallas_call(
        functools.partial(kernel, factors),
        out_shape=shapes,
        in_specs=[hbm] * 4,
        out_specs=(vmem,) * 4,
        scratch_shapes=[
            pltpu.VMEM((16, 4, 4, 128), BF16),
            pltpu.VMEM((27, 16, 32), BF16),
            pltpu.VMEM((1, 32), F32),
            pltpu.VMEM((32, 2, 2, 64), BF16),
            pltpu.VMEM((16, 4, 4, 128), F32),
            pltpu.VMEM((32, 2, 2, 64), F32),
            pltpu.VMEM((32, 2, 2, 64), F32),
            pltpu.VMEM((6, 6, 16, 128), BF16),
            pltpu.VMEM((2, 6, 6, 16, 128), BF16),
            pltpu.VMEM((4, 4, 512, 128), BF16),
            pltpu.VMEM((4, 4, 32, 128), F32),
            pltpu.VMEM((6, 6, 32, 128), BF16),
            pltpu.VMEM((4, 4, 288, 128), BF16),
            pltpu.VMEM((48, 288), BF16),
            pltpu.VMEM((16, 8, 128), F32),
            pltpu.VMEM((n_one, per, 8, 128), F32),
            pltpu.VMEM((n_two, per, 8, 128), F32),
            pltpu.VMEM((n_three, per, 8, 128), F32),
            pltpu.VMEM((16, 8, 128), F32),
            dma((4,)), dma((8,)), dma((8,)), dma((8,)), dma((8,)), dma((4,)), dma((4,)),
        ],
        compiler_params=pltpu.CompilerParams(
            collective_id=0, has_side_effects=True, vmem_limit_bytes=32 * 1024 * 1024),
        name="conv_step",
    )(*[pltpu.with_memory_space_constraint(v, pltpu.HBM)
        for v in (volume, weights.transpose(1, 2, 0), conv_bias.reshape(1, 32), pooled_grad)])
    pooled, vgrad, kgrad, bgrad = pl.pallas_call(
        leave,
        out_shape=shapes,
        in_specs=[vmem] * 4,
        out_specs=(pl.BlockSpec(memory_space=pltpu.HBM),) * 4,
        scratch_shapes=[dma((4,))],
        compiler_params=pltpu.CompilerParams(vmem_limit_bytes=1024 * 1024),
        name="leave",
    )(*outs)
    return (pooled, vgrad, kgrad.transpose(2, 0, 1), bgrad.reshape(32))


def solution(mesh):
    placed = (P(None, "block", "chan", None), P(), P(), P(None, "block", "chan", None))
    return jax.shard_map(
        functools.partial(local, factors_of(mesh)),
        mesh=mesh,
        in_specs=placed,
        out_specs=(P(None, "block", "chan", None), P(None, "block", "chan", None), P(), P()),
        check_vma=False,
    )
```

time: 56.4 us -> 47.5 us (0.84)
  local copies, waits for them, and re-layouts: 7.54 us -> 0 us
  Pallas kernels: 47.9 us -> 46.7 us
    unnamed x12 -> x0, local copies, waits for them, and re-layouts: 4.29 us -> none
    slice x2 -> x0, local copies, waits for them, and re-layouts: 1.51 us -> none  [the longest x1 0.82 us: local(): kgrad[:, :432].reshape(32, 27, 16)]
    pallas_call x1 -> x2, Pallas kernels: 47.9 us -> 46.7 us  [the longest x1 45.9 us: local(): pl.pallas_call(functools.partial(kernel, factors), out_shape=shapes, in_s...]
    reshape x3 -> x0, local copies, waits for them, and re-layouts: 1.17 us -> none  [the longest x1 0.96 us: local(): w5 = weights.reshape(32, 3, 3, 3, 16)[:, ::-1, ::-1, ::-1, :]]
where the time goes in v2:
time: 47.5 us; the launch traced here: 47.3 us
  Pallas kernels  46.7 us (98%)
  between operations  0.64 us (1%)
    pallas_call x1, Pallas kernels, local(): pl.pallas_call(functools.partial(kernel, factors), out_shape=shapes, in_s...  45.9 us

profile of v2, /device:TPU:1, one launch (start us, length us, event | category | flops | bytes accessed | tf_op | source)
XLA Modules:
  0.0 47.3 jit_solution(4225206752170775914)
XLA Ops:
  0.6 45.9 %conv_step.1 = (bf16[32,2,2,64]{3,2,1,0:T(2,128)(2,1)S(1)}, bf16[16,4,4,128]{3,2,1,0:T(4,128)(2,1)S(1)}, f32[27,16,32]{2,1,0:T(8,128)S(1)}, f32[1,32]{1,0:T(1,128)S(1)}) custom-call(bf16[16,4,4,128]{3,2,1,0:T(4,128)(2,1)} %volume_h.1, bf16[27,16,32]{2,1,0:T(8,128)(2,1)} %bitcast.4, f32[1,32]{1,0:T(1,128)} %bitcast.5, bf16[32,2,2,64]{3,2,1,0:T(2,128)(2,1)} %coarse_h.1), custom_call_target="tpu_custom_call" | custom-call | tf_op jit(solution)/shard_map/conv_step/pallas_call | solution.py:276
  46.6 0.7 %leave.1 = (bf16[32,2,2,64]{3,2,1,0:T(2,128)(2,1)}, bf16[16,4,4,128]{3,2,1,0:T(4,128)(2,1)}, f32[27,16,32]{2,1,0:T(8,128)}, f32[1,32]{1,0:T(1,128)}) custom-call(bf16[32,2,2,64]{3,2,1,0:T(2,128)(2,1)S(1)} %get-tuple-element.12.pooled_v, bf16[16,4,4,128]{3,2,1,0:T(4,128)(2,1)S(1)} %get-tuple-element.13.vgrad_v, f32[27,16,32]{2,1,0:T(8,128)S(1)} %get-tuple-element.14.kgrad_v, ...), custom_call_target="tpu_custom_call" | custom-call | tf_op jit(solution)/shard_map/leave/pallas_call | solution.py:308

commit v3 on v2

--- a/solution.py
+++ b/solution.py
@@ -10,7 +10,7 @@
 MESH = pl.DeviceIdType.MESH
 F32 = jnp.float32
 BF16 = jnp.bfloat16
-DIRECTIONS = [(i, j) for j in (-1, 1, 0) for i in (-1, 1, 0) if (i, j) != (0, 0)]
+DIRECTIONS = [(0, 1), (0, -1), (1, 0), (-1, 0), (1, 1), (1, -1), (-1, 1), (-1, -1)]
 
 
 def span_out(step):
@@ -53,10 +53,13 @@
     def inside(di, dj):
         return (blk + di >= 0) & (blk + di < nblock) & (chn + dj >= 0) & (chn + dj < nchan)
 
-    groups = ((n_one, me_one, dev_one), (n_two, me_two, dev_two), (n_three, me_three, dev_three))
+    groups = ((n_one, me_one, dev_one), (n_two, me_two, dev_two))
+    half = (n_three - 2) // 2
+    is_root = me_three < 2
+    first_served = jnp.where(me_three == 0, 2 + half, 2)
 
     barrier = pltpu.get_barrier_semaphore()
-    count = jnp.int32(n_one + n_two + n_three - 3)
+    count = n_one + n_two - 2 + jnp.where(is_root, 1, 2)
     for di, dj in DIRECTIONS:
         ok = inside(di, dj)
         count = count + ok.astype(jnp.int32)
@@ -68,9 +71,20 @@
         ((volume_h, volume_v), (weights_h, weights_v), (bias_h, bias_v), (coarse_h, coarse_v)))]
     for load in loads:
         load.start()
-    for n, me, dev in groups:
-        for k in far_first(n):
-            pl.semaphore_signal(barrier, inc=1, device_id=dev(lax.rem(me + k, n)), device_id_type=MESH)
+    def greet(device):
+        pl.semaphore_signal(barrier, inc=1, device_id=device, device_id_type=MESH)
+
+    for k in far_first(n_one):
+        greet(dev_one(lax.rem(me_one + k, n_one)))
+
+    for k in far_first(n_two):
+        greet(dev_two(lax.rem(me_two + k, n_two)))
+
+    @pl.when(is_root)
+    def _():
+        for k in far_first(n_three):
+            greet(dev_three(lax.rem(me_three + k, n_three)))
+
     loads[0].wait()
     vol_f[...] = volume_v[...].astype(F32)
     for i in range(4):
@@ -135,18 +149,38 @@
         w_back[16 * d:16 * d + 16, :] = jnp.concatenate(
             [weights_v[26 - 3 * s - d] for s in range(9)], axis=1)
 
-    halo_recv_wait(wide, halo_send, halo_recv)
-
-    for i in range(6):
-        moved = jnp.dot(wide[i].reshape(96, 128), shift_map, preferred_element_type=F32).astype(BF16)
-        shifted[0, i] = moved[:, :128].reshape(6, 16, 128)
-        shifted[1, i] = moved[:, 128:].reshape(6, 16, 128)
+    sources = (shifted.at[0], wide, shifted.at[1])
+
+    def shift(r0, r1, c0, c1):
+        shape = (r1 - r0, c1 - c0, 16, 128)
+        moved = jnp.dot(wide[r0:r1, c0:c1].reshape(-1, 128), shift_map, preferred_element_type=F32).astype(BF16)
+        shifted[0, r0:r1, c0:c1] = moved[:, :128].reshape(shape)
+        shifted[1, r0:r1, c0:c1] = moved[:, 128:].reshape(shape)
+
+    def gather(a, b, i0, i1, j0, j1):
+        for d in range(3):
+            t = 9 * a + 3 * b + d
+            cols[i0:i1, j0:j1, 16 * t:16 * t + 16, :] = sources[d][a + i0:a + i1, b + j0:b + j1]
+
+    own_part = ((1, 4), (0, 4), (0, 3))
+    rim_part = ((0, 1), None, (3, 4))
+    shift(1, 5, 1, 5)
     for a in range(3):
         for b in range(3):
-            for d in range(3):
-                t = 9 * a + 3 * b + d
-                source = wide if d == 1 else shifted.at[d // 2]
-                cols[:, :, 16 * t:16 * t + 16, :] = source[a:a + 4, b:b + 4]
+            gather(a, b, *own_part[a], *own_part[b])
+
+    halo_recv_wait(wide, halo_send, halo_recv)
+
+    shift(0, 1, 0, 6)
+    shift(5, 6, 0, 6)
+    shift(1, 5, 0, 1)
+    shift(1, 5, 5, 6)
+    for a in range(3):
+        for b in range(3):
+            if a != 1:
+                gather(a, b, *rim_part[a], 0, 4)
+            if b != 1:
+                gather(a, b, *own_part[a], *rim_part[b])
     for i in range(4):
         for j in range(4):
             act = jnp.dot(w_fwd, cols[i, j], preferred_element_type=F32) + bias
@@ -168,17 +202,14 @@
     per = 16 // n_one
     own = pl.ds(me_one * per, per)
 
-    def stage_copy(stage, group, k, src, dst):
-        n, me, dev = groups[group]
+    def copy_to(stage, device, src, dst):
         return pltpu.make_async_remote_copy(
             src_ref=src, dst_ref=dst, send_sem=stage_send.at[stage], recv_sem=stage_recv.at[stage],
-            device_id=dev(lax.rem(me + k, n)), device_id_type=MESH)
-
-    def stage_all(stage, buf, n):
-        ref = buf.at[pl.ds(0, n - 1)] if stage < 3 else buf.at[pl.ds(0, (n - 1) * per)]
-        return pltpu.make_async_remote_copy(
-            src_ref=ref, dst_ref=ref, send_sem=stage_send.at[stage], recv_sem=stage_recv.at[stage],
-            device_id=(blk, chn), device_id_type=MESH)
+            device_id=device, device_id_type=MESH)
+
+    def shards(stage, number):
+        ref = terms.at[pl.ds(0, number * per)] if number * per <= 16 else from_three.at[pl.ds(0, number)]
+        return copy_to(stage, (blk, chn), ref, ref)
 
     def total(buf, n):
         acc = buf[0]
@@ -187,65 +218,92 @@
         return acc
 
     for k in far_first(n_one):
-        stage_copy(0, 0, k, terms.at[pl.ds(lax.rem(me_one + k, n_one) * per, per)], from_one.at[me_one]).start()
+        other = lax.rem(me_one + k, n_one)
+        copy_to(0, dev_one(other), terms.at[pl.ds(other * per, per)], from_one.at[me_one]).start()
     from_one[me_one] = terms[own]
     halo_start(grad, grad_send, grad_recv)
     halo_send_wait(wide, halo_send, halo_recv)
 
-    stage_all(0, from_one, n_one).wait_recv()
+    shards(0, n_one - 1).wait_recv()
     from_two[me_two] = total(from_one, n_one)
     for k in far_first(n_two):
-        stage_copy(1, 1, k, from_two.at[me_two], from_two.at[me_two]).start()
+        copy_to(2, dev_two(lax.rem(me_two + k, n_two)), from_two.at[me_two], from_two.at[me_two]).start()
 
     pool_row = lax.broadcasted_iota(jnp.int32, (128, 64), 0)
     pool_lane = lax.broadcasted_iota(jnp.int32, (128, 64), 1)
     pool_map = jnp.where(lax.shift_right_logical(pool_row, 1) == pool_lane, 0.125, 0.0).astype(F32)
+    def smooth_row(i, carry):
+        v = pre[i]
+        pre[i] = 0.2 * v + 0.8 * (jnp.maximum(v, 0.0) + jnp.log1p(jnp.exp(-jnp.abs(v))))
+        return carry
+
+    lax.fori_loop(0, 4, smooth_row, 0)
+    sums = jnp.concatenate([pre[2 * i, 2 * j] + pre[2 * i, 2 * j + 1] + pre[2 * i + 1, 2 * j] + pre[2 * i + 1, 2 * j + 1]
+                            for i in range(2) for j in range(2)], axis=0)
+    means = jnp.dot(sums, pool_map, precision=lax.Precision.HIGHEST, preferred_element_type=F32)
     for i in range(2):
         for j in range(2):
-            acc = None
-            for p in range(2):
-                for q in range(2):
-                    v = pre[2 * i + p, 2 * j + q]
-                    smooth = 0.2 * v + 0.8 * (jnp.maximum(v, 0.0) + jnp.log1p(jnp.exp(-jnp.abs(v))))
-                    acc = smooth if acc is None else acc + smooth
-            pool_f[:, i, j, :] = jnp.dot(acc, pool_map, precision=lax.Precision.HIGHEST, preferred_element_type=F32)
+            pool_f[:, i, j, :] = means[64 * i + 32 * j:64 * i + 32 * j + 32]
     pooled_o[...] = pool_f[...].astype(BF16)
-    stage_all(0, from_one, n_one).wait_send()
-
-    stage_all(1, from_two, n_two).wait_recv()
+    shards(0, n_one - 1).wait_send()
+
+    shards(2, n_two - 1).wait_recv()
     from_three[me_three] = total(from_two, n_two)
-    for k in far_first(n_three):
-        stage_copy(2, 2, k, from_three.at[me_three], from_three.at[me_three]).start()
-
-    stage_all(1, from_two, n_two).wait_send()
+    for root in range(2):
+        @pl.when(me_three != root)
+        def _(root=root):
+            copy_to(1, dev_three(root), from_three.at[me_three], from_three.at[me_three]).start()
+    shards(2, n_two - 1).wait_send()
+
     halo_recv_wait(grad, grad_send, grad_recv)
     for a in range(3):
         for b in range(3):
             t = 3 * a + b
             cols_back[:, :, 32 * t:32 * t + 32, :] = grad[a:a + 4, b:b + 4]
     zlane = lax.broadcasted_iota(jnp.int32, (16, 128), 1)
-    for i in range(4):
+    def back_row(i, carry):
         for j in range(4):
             part = jnp.dot(w_back[...], cols_back[i, j], preferred_element_type=F32)
             before = jnp.where(zlane == 0, 0.0, pltpu.roll(part[:16], 1, 1))
             after = jnp.where(zlane == 127, 0.0, pltpu.roll(part[32:], 127, 1))
             vol_f[:, i, j, :] = before + part[16:32] + after
+        return carry
+
+    lax.fori_loop(0, 4, back_row, 0)
     vgrad_o[...] = vol_f[...].astype(BF16)
     halo_send_wait(grad, grad_send, grad_recv)
 
-    stage_all(2, from_three, n_three).wait_recv()
-    result[own] = total(from_three, n_three)
+    @pl.when(is_root)
+    def _():
+        shards(1, 1).wait_send()
+        shards(1, n_three - 1).wait_recv()
+        result[own] = total(from_three, n_three)
+
+    @pl.when(jnp.logical_not(is_root))
+    def _():
+        shards(1, 2).wait_send()
+        shards(4, 1).wait_recv()
+
     for k in far_first(n_one):
-        stage_copy(3, 0, k, result.at[own], result.at[own]).start()
-    stage_all(2, from_three, n_three).wait_send()
-    stage_all(3, result, n_one).wait_recv()
+        copy_to(3, dev_one(lax.rem(me_one + k, n_one)), result.at[own], result.at[own]).start()
+
+    @pl.when(is_root)
+    def _():
+        for k in range(half):
+            copy_to(4, dev_three(first_served + k), result.at[own], result.at[own]).start()
+
+    shards(3, n_one - 1).wait_recv()
     full = result[...].reshape(128, 128)
     for q in range(4):
         part = full if q == 0 else pltpu.roll(full, 128 - 32 * q, 1)
         taps = 8 if q < 3 else 3
         kgrad_o[8 * q:8 * q + taps] = part[:16 * taps, :32].reshape(taps, 16, 32)
     bgrad_o[...] = part[48:49, :32]
-    stage_all(3, result, n_one).wait_send()
+    shards(3, n_one - 1).wait_send()
+
+    @pl.when(is_root)
+    def _():
+        shards(4, half).wait_send()
 
 
 def leave(pooled_v, vgrad_v, kgrad_v, bgrad_v, pooled_h, vgrad_h, kgrad_h, bgrad_h, sem):
@@ -298,7 +356,7 @@
             pltpu.VMEM((n_two, per, 8, 128), F32),
             pltpu.VMEM((n_three, per, 8, 128), F32),
             pltpu.VMEM((16, 8, 128), F32),
-            dma((4,)), dma((8,)), dma((8,)), dma((8,)), dma((8,)), dma((4,)), dma((4,)),
+            dma((4,)), dma((8,)), dma((8,)), dma((8,)), dma((8,)), dma((5,)), dma((5,)),
         ],
         compiler_params=pltpu.CompilerParams(
             collective_id=0, has_side_effects=True, vmem_limit_bytes=32 * 1024 * 1024),

time: 47.5 us -> 46.6 us (0.981)
  Pallas kernels: 46.7 us -> 45.8 us
    pallas_call x1, Pallas kernels: 45.9 us -> 45.1 us  [local(): pl.pallas_call(functools.partial(kernel, factors), out_shape=shapes, in_s...]
where the time goes in v3:
time: 46.6 us; the launch traced here: 46.5 us
  Pallas kernels  45.8 us (98%)
  between operations  0.64 us (1%)
    pallas_call x1, Pallas kernels, local(): pl.pallas_call(functools.partial(kernel, factors), out_shape=shapes, in_s...  45.1 us

profile of v3, /device:TPU:1, one launch (start us, length us, event | category | flops | bytes accessed | tf_op | source)
XLA Modules:
  0.0 46.5 jit_solution(5981283585445531344)
XLA Ops:
  0.6 45.1 %conv_step.1 = (bf16[32,2,2,64]{3,2,1,0:T(2,128)(2,1)S(1)}, bf16[16,4,4,128]{3,2,1,0:T(4,128)(2,1)S(1)}, f32[27,16,32]{2,1,0:T(8,128)S(1)}, f32[1,32]{1,0:T(1,128)S(1)}) custom-call(bf16[16,4,4,128]{3,2,1,0:T(4,128)(2,1)} %volume_h.1, bf16[27,16,32]{2,1,0:T(8,128)(2,1)} %bitcast.4, f32[1,32]{1,0:T(1,128)} %bitcast.5, bf16[32,2,2,64]{3,2,1,0:T(2,128)(2,1)} %coarse_h.1), custom_call_target="tpu_custom_call" | custom-call | tf_op jit(solution)/shard_map/conv_step/pallas_call | solution.py:334
  45.7 0.7 %leave.1 = (bf16[32,2,2,64]{3,2,1,0:T(2,128)(2,1)}, bf16[16,4,4,128]{3,2,1,0:T(4,128)(2,1)}, f32[27,16,32]{2,1,0:T(8,128)}, f32[1,32]{1,0:T(1,128)}) custom-call(bf16[32,2,2,64]{3,2,1,0:T(2,128)(2,1)S(1)} %get-tuple-element.12.pooled_v, bf16[16,4,4,128]{3,2,1,0:T(4,128)(2,1)S(1)} %get-tuple-element.13.vgrad_v, f32[27,16,32]{2,1,0:T(8,128)S(1)} %get-tuple-element.14.kgrad_v, ...), custom_call_target="tpu_custom_call" | custom-call | tf_op jit(solution)/shard_map/leave/pallas_call | solution.py:366

commit v4 on v3

--- a/solution.py
+++ b/solution.py
@@ -67,16 +67,16 @@
         @pl.when(ok)
         def _(di=di, dj=dj):
             pl.semaphore_signal(barrier, inc=1, device_id=(blk + di, chn + dj), device_id_type=MESH)
+    def greet(device):
+        pl.semaphore_signal(barrier, inc=1, device_id=device, device_id_type=MESH)
+
+    for k in far_first(n_one):
+        greet(dev_one(lax.rem(me_one + k, n_one)))
+
     loads = [pltpu.make_async_copy(src, dst, in_sem.at[i]) for i, (src, dst) in enumerate(
         ((volume_h, volume_v), (weights_h, weights_v), (bias_h, bias_v), (coarse_h, coarse_v)))]
     for load in loads:
         load.start()
-    def greet(device):
-        pl.semaphore_signal(barrier, inc=1, device_id=device, device_id_type=MESH)
-
-    for k in far_first(n_one):
-        greet(dev_one(lax.rem(me_one + k, n_one)))
-
     for k in far_first(n_two):
         greet(dev_two(lax.rem(me_two + k, n_two)))
 

time: 46.6 us -> 46.6 us (level)
  no operation moved by 1% of the time
where the time goes in v4:
time: 46.6 us; the launch traced here: 46.4 us
  Pallas kernels  45.8 us (98%)
  between operations  0.64 us (1%)
    pallas_call x1, Pallas kernels, local(): pl.pallas_call(functools.partial(kernel, factors), out_shape=shapes, in_s...  45.1 us

profile of v4, /device:TPU:1, one launch (start us, length us, event | category | flops | bytes accessed | tf_op | source)
XLA Modules:
  0.0 46.4 jit_solution(3787639991031645225)
XLA Ops:
  0.6 45.1 %conv_step.1 = (bf16[32,2,2,64]{3,2,1,0:T(2,128)(2,1)S(1)}, bf16[16,4,4,128]{3,2,1,0:T(4,128)(2,1)S(1)}, f32[27,16,32]{2,1,0:T(8,128)S(1)}, f32[1,32]{1,0:T(1,128)S(1)}) custom-call(bf16[16,4,4,128]{3,2,1,0:T(4,128)(2,1)} %volume_h.1, bf16[27,16,32]{2,1,0:T(8,128)(2,1)} %bitcast.4, f32[1,32]{1,0:T(1,128)} %bitcast.5, bf16[32,2,2,64]{3,2,1,0:T(2,128)(2,1)} %coarse_h.1), custom_call_target="tpu_custom_call" | custom-call | tf_op jit(solution)/shard_map/conv_step/pallas_call | solution.py:334
  45.7 0.7 %leave.1 = (bf16[32,2,2,64]{3,2,1,0:T(2,128)(2,1)}, bf16[16,4,4,128]{3,2,1,0:T(4,128)(2,1)}, f32[27,16,32]{2,1,0:T(8,128)}, f32[1,32]{1,0:T(1,128)}) custom-call(bf16[32,2,2,64]{3,2,1,0:T(2,128)(2,1)S(1)} %get-tuple-element.12.pooled_v, bf16[16,4,4,128]{3,2,1,0:T(4,128)(2,1)S(1)} %get-tuple-element.13.vgrad_v, f32[27,16,32]{2,1,0:T(8,128)S(1)} %get-tuple-element.14.kgrad_v, ...), custom_call_target="tpu_custom_call" | custom-call | tf_op jit(solution)/shard_map/leave/pallas_call | solution.py:366

commit v5 on v3

--- a/solution.py
+++ b/solution.py
@@ -226,8 +226,10 @@
 
     shards(0, n_one - 1).wait_recv()
     from_two[me_two] = total(from_one, n_one)
-    for k in far_first(n_two):
-        copy_to(2, dev_two(lax.rem(me_two + k, n_two)), from_two.at[me_two], from_two.at[me_two]).start()
+    for r in range(n_two):
+        @pl.when(me_two != r)
+        def _(r=r):
+            copy_to(2, dev_two(r), from_two.at[me_two], from_two.at[me_two]).start()
 
     pool_row = lax.broadcasted_iota(jnp.int32, (128, 64), 0)
     pool_lane = lax.broadcasted_iota(jnp.int32, (128, 64), 1)

time: 46.6 us -> 46.5 us (level)
  no operation moved by 1% of the time
where the time goes in v5:
time: 46.5 us; the launch traced here: 46.3 us
  Pallas kernels  45.7 us (98%)
  between operations  0.64 us (1%)
    pallas_call x1, Pallas kernels, local(): pl.pallas_call(functools.partial(kernel, factors), out_shape=shapes, in_s...  45 us

profile of v5, /device:TPU:1, one launch (start us, length us, event | category | flops | bytes accessed | tf_op | source)
XLA Modules:
  0.0 46.3 jit_solution(1894151838147808121)
XLA Ops:
  0.6 45.0 %conv_step.1 = (bf16[32,2,2,64]{3,2,1,0:T(2,128)(2,1)S(1)}, bf16[16,4,4,128]{3,2,1,0:T(4,128)(2,1)S(1)}, f32[27,16,32]{2,1,0:T(8,128)S(1)}, f32[1,32]{1,0:T(1,128)S(1)}) custom-call(bf16[16,4,4,128]{3,2,1,0:T(4,128)(2,1)} %volume_h.1, bf16[27,16,32]{2,1,0:T(8,128)(2,1)} %bitcast.4, f32[1,32]{1,0:T(1,128)} %bitcast.5, bf16[32,2,2,64]{3,2,1,0:T(2,128)(2,1)} %coarse_h.1), custom_call_target="tpu_custom_call" | custom-call | tf_op jit(solution)/shard_map/conv_step/pallas_call | solution.py:336
  45.6 0.7 %leave.1 = (bf16[32,2,2,64]{3,2,1,0:T(2,128)(2,1)}, bf16[16,4,4,128]{3,2,1,0:T(4,128)(2,1)}, f32[27,16,32]{2,1,0:T(8,128)}, f32[1,32]{1,0:T(1,128)}) custom-call(bf16[32,2,2,64]{3,2,1,0:T(2,128)(2,1)S(1)} %get-tuple-element.12.pooled_v, bf16[16,4,4,128]{3,2,1,0:T(4,128)(2,1)S(1)} %get-tuple-element.13.vgrad_v, f32[27,16,32]{2,1,0:T(8,128)S(1)} %get-tuple-element.14.kgrad_v, ...), custom_call_target="tpu_custom_call" | custom-call | tf_op jit(solution)/shard_map/leave/pallas_call | solution.py:368
